TPU v7x, 128 devices: a whole 4x4x4 slice. The times are simulated.
128 devices in a mesh: net: 8 (over z, core), strip: 16 (over y, x).
Axes of the slice: x: 4, y: 4, z: 4, core: 2. Of those that a mesh axis runs over, the one named last changes fastest.
Arguments:
- cond_charge: bfloat16 [3072, 32, 128], P(('net', 'strip')), may hold values from -6 to 6
- cond_live: int32 [128], P(('net', 'strip')), may hold values from 2 to 24, as said below
- near_src: int32 [3072, 16], P(('net', 'strip')), may hold values from -1 to 3071, as said below
- near_mat: bfloat16 [3072, 16, 128, 128], P(('net', 'strip')), may hold values from -0.125 to 0.125
- cond_basis: bfloat16 [3072, 16, 128], P(('net', 'strip')), may hold values from -0.5 to 0.5
- cond_rank: int32 [3072], P(('net', 'strip')), may hold values from 8 to 16
- far_src: int32 [3072, 16], P(('net', 'strip')), may hold values from -1 to 3583, as said below
- far_mat: bfloat16 [3072, 16, 16, 16], P(('net', 'strip')), may hold values from -0.375 to 0.375
- iface_charge: bfloat16 [512, 32, 128], P('strip', 'net'), may hold values from -6 to 6
- iface_near: bfloat16 [512, 3, 128, 128], P('strip'), may hold values from -0.3125 to 0.3125
- iface_basis: bfloat16 [512, 16, 128], P('strip'), may hold values from -0.5 to 0.5
- iface_rank: int32 [512], P('strip'), may hold values from 8 to 16
- iface_far_src: int32 [512, 16], P('strip'), may hold values from -1 to 3583, as said below
- iface_far_mat: bfloat16 [512, 16, 16, 16], P('strip'), may hold values from -0.375 to 0.375
Outputs:
- cond_pot: bfloat16 [3072, 32, 128], P(('net', 'strip'))
- iface_pot: bfloat16 [512, 32, 128], P('strip', 'net')
Inputs may be any that keep to these rules, and one draw needn't show every extreme that they name: `cond_live`: in every draw, two devices of every net group have all 24 slots live; live slots are the first ones of a device. `near_src`: entry 0 of a row is the row's own block. Every other entry is -1 (padding, only after the used entries) or a live conductor slot of a device with the same net index as the row's device. `far_src`: each entry is -1 (padding, only after the used entries), a live conductor slot, or an interface block number. `iface_far_src`: each entry is -1 (padding, only after the used entries), a live conductor slot, or an interface block number.
All inputs are finite; a program needn't handle non-finite values.
Results may differ from a plain program's by a relative error of at most 0.0027.
Values may be sent and summed in bfloat16 or wider, within the bound.
No kernel may reach another device: no remote copies, remote signals or barrier semaphores. Data moves between devices by JAX's collectives and lax.ppermute only.
A program may use at most 128 MiB of HBM per device.

v0:
```python
import jax
import jax.numpy as jnp
from jax import lax
from jax.sharding import PartitionSpec as P


def extended(array, sides, width):
    for axis, dim in sides:
        peers, length = (lax.axis_size(axis), array.shape[dim])
        up = [(i, (i + 1) % peers) for i in range(peers - 1)]
        down = [(j, i) for i, j in up]
        last = lax.slice_in_dim(array, length - width, length, axis=dim)
        leading = lax.slice_in_dim(array, 0, width, axis=dim)
        before = lax.ppermute(last, axis, up)
        after = lax.ppermute(leading, axis, down)
        array = jnp.concatenate([before, array, after], axis=dim)
    return array


def coeffs(block_basis, charge, block_rank):
    product = jnp.einsum("tap,trp->tar", block_basis, charge, preferred_element_type=jnp.float32)
    keep_rows = (jnp.arange(block_basis.shape[1])[None, :] < block_rank[:, None]).astype(
        jnp.float32
    )
    return (product * keep_rows[:, :, None]).astype(jnp.bfloat16)


def far_field(source_ids, far_mats, block_basis, block_rank, coef_table):
    usable = (source_ids >= 0).astype(jnp.bfloat16)
    fetched = coef_table[jnp.maximum(source_ids, 0)] * usable[:, :, None, None]
    gathered_far = jnp.einsum(
        "tkab,tkbr->tar", far_mats, fetched, preferred_element_type=jnp.float32
    )
    keep_rows = (jnp.arange(block_basis.shape[1])[None, :] < block_rank[:, None]).astype(
        jnp.float32
    )
    gathered_far = (gathered_far * keep_rows[:, :, None]).astype(jnp.bfloat16)
    return jnp.einsum("tap,tar->trp", block_basis, gathered_far, preferred_element_type=jnp.float32)


def shards(
    cond_charge,
    cond_live,
    near_src,
    near_mat,
    cond_basis,
    cond_rank,
    far_src,
    far_mat,
    iface_charge,
    iface_near,
    iface_basis,
    iface_rank,
    iface_far_src,
    iface_far_mat,
):
    cond_blocks = cond_charge.shape[0]
    iface_blocks = iface_charge.shape[0]
    excite_rows = iface_charge.shape[1]
    strip_count = lax.axis_size("strip")
    net_index = lax.axis_index("net")
    grouped = lax.all_gather(cond_charge, "strip", axis=0, tiled=True)
    local_ids = near_src - net_index * strip_count * cond_blocks
    usable = (near_src >= 0).astype(jnp.bfloat16)
    fetched = grouped[jnp.clip(local_ids, 0, grouped.shape[0] - 1)] * usable[:, :, None, None]
    near_part = jnp.einsum("tkpq,tkrq->trp", near_mat, fetched, preferred_element_type=jnp.float32)
    rimmed = extended(iface_charge, (("strip", 0),), 1)
    iface_near_part = jnp.einsum(
        "tpq,trq->trp", iface_near[:, 0], rimmed[:iface_blocks], preferred_element_type=jnp.float32
    )
    iface_near_part = iface_near_part + jnp.einsum(
        "tpq,trq->trp",
        iface_near[:, 1],
        rimmed[1 : iface_blocks + 1],
        preferred_element_type=jnp.float32,
    )
    iface_near_part = iface_near_part + jnp.einsum(
        "tpq,trq->trp", iface_near[:, 2], rimmed[2:], preferred_element_type=jnp.float32
    )
    cond_coef = coeffs(cond_basis, cond_charge, cond_rank)
    iface_local = coeffs(iface_basis, iface_charge, iface_rank)
    iface_full = lax.all_gather(iface_local, "net", axis=2, tiled=True)
    cond_table = lax.all_gather(cond_coef, ("net", "strip"), axis=0, tiled=True)
    iface_table = lax.all_gather(iface_full, "strip", axis=0, tiled=True)
    coef_table = jnp.concatenate([cond_table, iface_table], 0)
    cond_far = far_field(far_src, far_mat, cond_basis, cond_rank, coef_table)
    excite_table = lax.dynamic_slice_in_dim(coef_table, net_index * excite_rows, excite_rows, 2)
    iface_far = far_field(iface_far_src, iface_far_mat, iface_basis, iface_rank, excite_table)
    alive_mask = (jnp.arange(cond_blocks) < cond_live[0]).astype(jnp.float32)
    cond_pot = ((near_part + cond_far) * alive_mask[:, None, None]).astype(jnp.bfloat16)
    iface_pot = (iface_near_part + iface_far).astype(jnp.bfloat16)
    return (cond_pot, iface_pot)


def solution(mesh):
    placed = (
        P(("net", "strip"), None, None),
        P(("net", "strip")),
        P(("net", "strip"), None),
        P(("net", "strip"), None, None, None),
        P(("net", "strip"), None, None),
        P(("net", "strip")),
        P(("net", "strip"), None),
        P(("net", "strip"), None, None, None),
        P("strip", "net", None),
        P("strip", None, None, None),
        P("strip", None, None),
        P("strip"),
        P("strip", None),
        P("strip", None, None, None),
    )
    return jax.shard_map(
        shards,
        mesh=mesh,
        in_specs=placed,
        out_specs=(P(("net", "strip"), None, None), P("strip", "net", None)),
        check_vma=False,
    )
```

profile of v0, /device:TPU:1, one launch (start us, length us, event | category | flops | bytes accessed | tf_op | source)
XLA Modules:
  0.0 214.6 jit_solution(11559196575613654127)
XLA Ops:
  7.2 0.0 copy-start
  7.2 0.0 copy-start.7
  7.2 0.0 copy-start.9
  7.2 0.0 copy-start.11
  7.2 0.0 copy-start.10
  7.2 0.0 copy-start.4
  7.2 0.0 all-gather.3.cloned.1.call-start
  7.3 0.7 all-gather.3.cloned.1.call-update
  8.0 0.0 all-gather.5.cloned.1.call-start
  8.0 0.7 fusion.50
  8.7 1.8 fusion.19
  10.6 0.0 all-gather.5.cloned.1.call-update
  10.6 0.7 fusion.53
  11.3 1.3 collective-permute-start.1
  12.6 4.6 %collective-permute-start = (bf16[1,4,128]{2,1,0:T(4,128)(2,1)S(1)}, bf16[1,4,128]{2,1,0:T(4,128)(2,1)S(1)}, u32[]{:S(2)}, u32[]{:S(2)}) collective-permute-start(bf16[1,4,128]{2,1,0:T(4,128)(2,1)S(1)} %get-tuple-element.2), channel_id=1, source_target_pairs={{0,1},{1,2},{2,3},{3,4},{4,5},{5,6},{6,7},{7,8},{8,9},{9,10},{10,1... | collective-permute-start | bytes 3080 | tf_op jit(solution)/shard_map/ppermute | solution.py:14
  17.2 0.7 fusion.49
  17.9 0.0 copy-done
  17.9 0.9 fusion.27
  18.8 0.1 copy.71
  18.9 15.3 %all_gather.14 = bf16[32,16,32]{0,1,2:T(8,128)(2,1)S(1)} all-gather(bf16[32,16,4]{0,1,2:T(8,128)(2,1)S(1)} %copy.71), channel_id=1, replica_groups=mesh['net'=8,'strip'=16] {'net'}, dimensions={2}, use_global_device_ids=true | all-gather | bytes 36864 | tf_op jit(solution)/shard_map/all_gather | solution.py:82
  34.2 0.2 copy.72
  34.4 0.7 broadcast_maximum_fusion
  35.1 0.1 copy.79
  35.2 0.1 reshape.74
  35.3 0.7 broadcast_maximum_fusion.1
  36.0 0.1 copy.73
  36.0 0.1 reshape.66
  36.1 0.7 compare_select_fusion
  36.8 0.1 copy.69
  36.9 0.1 reshape.58
  37.7 0.0 copy-start.5
  37.7 32.7 %all_gather.15 = bf16[512,16,32]{2,1,0:T(8,128)(2,1)} all-gather(bf16[32,16,32]{2,1,0:T(8,128)(2,1)S(1)} %copy.72), channel_id=1, replica_groups=mesh['net'=8,'strip'=16] {'strip'}, dimensions={0}, use_global_device_ids=true | all-gather | bytes 557056 | tf_op jit(solution)/shard_map/all_gather | solution.py:84
  70.4 0.0 copy-done.9
  70.4 0.0 copy-done.10
  70.4 0.0 copy-done.11
  70.4 0.0 copy-done.7
  70.5 1.9 fusion.31
  72.3 0.1 copy.82
  72.4 0.0 copy-done.4
  72.4 4.4 %copy.84 = bf16[32,16,16,16]{2,1,3,0:T(8,128)(2,1)} copy(bf16[32,16,16,16]{0,3,2,1:T(8,128)(2,1)S(1)} %copy-done.4) | data formatting | bytes 524288 | tf_op args[13]
  76.8 0.1 copy.70
  76.9 0.0 copy-done.5
  76.9 3.5 %copy.75 = bf16[24,16,16,16]{3,2,1,0:T(8,128)(2,1)} copy(bf16[24,16,16,16]{0,3,2,1:T(8,128)(2,1)S(1)} %copy-done.5) | data formatting | bytes 393216 | tf_op args[7]
  80.3 0.1 copy.74
  80.4 0.0 collective-permute-done.1
  80.4 1.9 fusion.29
  82.3 3.2 %gather_fusion = bf16[384,32,128]{2,1,0:T(8,128)(2,1)S(1)} fusion(bf16[384,32,128]{2,1,0:T(8,128)(2,1)} %all-gather.3.cloned.1.call-done, s32[1024]{0:T(1024)S(1)} %pad_clamp_fusion.2), kind=kCustom, calls=%fused_computation | custom fusion | bytes 6292992 | tf_op jit(solution)/shard_map/gather | solution.py:65
  85.5 8.0 %fusion.6 = f32[24,32,128]{2,1,0:T(8,128)} fusion(bf16[24,16,128,128]{3,2,1,0:T(8,128)(2,1)} %param.17, bf16[24,16,32,128]{3,2,1,0:T(8,128)(2,1)S(1)} %bitcast.52, bf16[24,16]{1,0:T(8,128)(2,1)S(1)} %copy.70), kind=kOutput, calls=%fused_computation.10 | convolution fusion | flops 404226048 | bytes 16122624 | tf_op jit(solution)/shard_map/tkpq,tkrq->trp/dot_general | solution.py:66
  93.5 50.7 %all-gather.5.cloned.1.call-done = bf16[3072,16,32]{2,1,0:T(8,128)(2,1)} async-done(((bf16[24,16,32]{2,1,0:T(8,128)(2,1)}), bf16[3072,16,32]{2,1,0:T(8,128)(2,1)}) %all-gather.5.cloned.1.call-update) | async-done | bytes 3145744 | tf_op jit(solution)/shard_map/all_gather | solution.py:83
  144.2 6.8 %constant_dynamic-update-slice_fusion.1 = bf16[3584,16,32]{2,1,0:T(8,128)(2,1)S(1)} fusion(bf16[3072,16,32]{2,1,0:T(8,128)(2,1)} %all-gather.5.cloned.1.call-done), kind=kLoop, calls=%fused_computation.58 | loop fusion | bytes 15728640
  151.0 0.0 copy-done.2
  151.0 0.5 constant_dynamic-update-slice_fusion
  151.5 0.0 copy-start.1
  151.6 5.2 %copy-done.1 = bf16[3584,16,32]{2,1,0:T(8,128)(2,1)} copy-done((bf16[3584,16,32]{2,1,0:T(8,128)(2,1)}, bf16[3584,16,32]{2,1,0:T(8,128)(2,1)S(1)}, u32[]{:S(2)}) %copy-start.1) | copy-done | bytes 3670040
  156.8 7.8 %constant_dynamic-slice_fusion = bf16[3584,16,4]{2,1,0:T(8,128)(2,1)} fusion(bf16[3584,16,32]{2,1,0:T(8,128)(2,1)S(1)} %constant_dynamic-update-slice_fusion, s32[]{:T(128)S(6)} %select_n.9), kind=kLoop, calls=%fused_computation.62 | loop fusion | bytes 917508 | tf_op jit(solution)/shard_map/dynamic_slice | solution.py:87
  164.6 24.0 %copy.80 = bf16[3584,16,4]{1,2,0:T(4,128)(2,1)} copy(bf16[3584,16,4]{2,1,0:T(8,128)(2,1)} %constant_dynamic-slice_fusion) | data formatting | bytes 917504 | tf_op jit(solution)/shard_map/dynamic_slice | solution.py:87
  188.6 3.5 %gather_fusion.2 = bf16[512,16,4]{1,2,0:T(4,128)(2,1)S(1)} fusion(bf16[3584,16,4]{1,2,0:T(4,128)(2,1)} %copy.80, s32[1024]{0:T(1024)S(1)} %pad_clamp_fusion), kind=kCustom, calls=%fused_computation.2 | custom fusion | bytes 133120 | tf_op jit(solution)/shard_map/gather | solution.py:30
  192.2 0.0 copy-start.8
  192.2 0.9 copy.88
  193.1 7.2 %gather_fusion.1 = bf16[384,16,32]{2,1,0:T(8,128)(2,1)} fusion(bf16[3584,16,32]{2,1,0:T(8,128)(2,1)} %copy-done.1, s32[1024]{0:T(1024)S(1)} %pad_clamp_fusion.1), kind=kCustom, calls=%fused_computation.1 | custom fusion | bytes 787968 | tf_op jit(solution)/shard_map/gather | solution.py:30
  200.4 3.9 %fusion.9 = bf16[24,32,128]{2,1,0:T(8,128)(2,1)} fusion(f32[24,32,128]{2,1,0:T(8,128)S(1)} %copy-done.6, bf16[24,16,128]{2,1,0:T(8,128)(2,1)S(1)} %copy-done.8, bf16[24,16,16,16]{3,2,1,0:T(8,128)(2,1)} %copy.75, bf16[24,16,16,32]{3,2,1,0:T(8,128)(2,1)} %bitcast.53, bf16[24,16]{1,0:T(8,128)(2,1)S(1)} %copy.74, f32[24]{0:T(128)S(1)} %compare_convert_fusion.3, ...), kind=kOutput, calls=%fused_computation.11 | convolution fusion | flops 10543104 | bytes 1280352 | tf_op jit(solution)/shard_map/tap,tar->trp/dot_general | solution.py:38
  204.3 0.9 fusion.28
  205.2 0.0 collective-permute-done
  205.2 2.5 %fusion.25 = bf16[32,4,128]{2,1,0:T(4,128)(2,1)} fusion(f32[32,4,128]{2,1,0:T(4,128)S(1)} %fusion.28, f32[32,4,128]{2,1,0:T(4,128)S(1)} %fusion.29, f32[32,4,128]{2,1,0:T(4,128)S(1)} %fusion.31, bf16[32,3,128,128]{3,2,1,0:T(8,128)(2,1)} %param.23, bf16[32,4,128]{2,1,0:T(4,128)(2,1)S(1)} %copy-done.7, bf16[1,4,128]{2,1,0:T(4,128)(2,1)S(1)} %collective-permute-done), kind=kOutput, calls=%fused_computation.23 | convolution fusion | flops 4327424 | bytes 1311744 | tf_op jit(solution)/shard_map/tpq,trq->trp/dot_general | solution.py:68
  (15 shorter events, 0.1 us)
Async XLA Ops:
  7.2 10.7 %copy-start = (bf16[32,16,128]{2,1,0:T(8,128)(2,1)S(1)}, bf16[32,16,128]{2,1,0:T(8,128)(2,1)}, u32[]{:S(2)}) copy-start(bf16[32,16,128]{2,1,0:T(8,128)(2,1)} %param.24) | copy-start | bytes 393220
  7.2 63.3 %copy-start.7 = (bf16[32,4,128]{2,1,0:T(4,128)(2,1)S(1)}, bf16[32,4,128]{2,1,0:T(4,128)(2,1)}, u32[]{:S(2)}) copy-start(bf16[32,4,128]{2,1,0:T(4,128)(2,1)} %param.22) | copy-start | bytes 98308
  7.2 63.2 %copy-start.9 = (s32[32,16]{0,1:T(8,128)S(1)}, s32[32,16]{0,1:T(8,128)}, u32[]{:S(2)}) copy-start(s32[32,16]{0,1:T(8,128)} %param.26) | copy-start | bytes 6148
  7.2 63.2 %copy-start.11 = (s32[24,16]{0,1:T(8,128)S(1)}, s32[24,16]{0,1:T(8,128)}, u32[]{:S(2)}) copy-start(s32[24,16]{0,1:T(8,128)} %param.20) | copy-start | bytes 4612
  7.2 63.2 %copy-start.10 = (s32[24,16]{0,1:T(8,128)S(1)}, s32[24,16]{0,1:T(8,128)}, u32[]{:S(2)}) copy-start(s32[24,16]{0,1:T(8,128)} %param.16) | copy-start | bytes 4612
  7.2 65.2 %copy-start.4 = (bf16[32,16,16,16]{0,3,2,1:T(8,128)(2,1)S(1)}, bf16[32,16,16,16]{0,3,2,1:T(8,128)(2,1)}, u32[]{:S(2)}) copy-start(bf16[32,16,16,16]{0,3,2,1:T(8,128)(2,1)} %param.27) | copy-start | bytes 786436
  7.2 75.1 %all-gather.3.cloned.1.call-start = ((), (), s32[]{:S(2)}) async-start(), calls=%async_computation | async-start | bytes 3342336 | tf_op jit(solution)/shard_map/all_gather | solution.py:62
  8.0 136.2 %all-gather.5.cloned.1.call-start = ((), (), s32[]{:S(2)}) async-start(), calls=%async_computation.1 | async-start | bytes 12681216 | tf_op jit(solution)/shard_map/all_gather | solution.py:83
  11.3 69.1 %collective-permute-start.1 = (bf16[1,4,128]{2,1,0:T(4,128)(2,1)S(1)}, bf16[1,4,128]{2,1,0:T(4,128)(2,1)S(1)}, u32[]{:S(2)}, u32[]{:S(2)}) collective-permute-start(bf16[1,4,128]{2,1,0:T(4,128)(2,1)S(1)} %get-tuple-element.3), channel_id=1, source_target_pairs={{1,0},{2,1},{3,2},{4,3},{5,4},{6,5},{7,6},{8,7},{9,8},{10,9},{11,1... | collective-permute-start | bytes 3080 | tf_op jit(solution)/shard_map/ppermute | solution.py:15
  12.6 192.6 %collective-permute-start = (bf16[1,4,128]{2,1,0:T(4,128)(2,1)S(1)}, bf16[1,4,128]{2,1,0:T(4,128)(2,1)S(1)}, u32[]{:S(2)}, u32[]{:S(2)}) collective-permute-start(bf16[1,4,128]{2,1,0:T(4,128)(2,1)S(1)} %get-tuple-element.2), channel_id=1, source_target_pairs={{0,1},{1,2},{2,3},{3,4},{4,5},{5,6},{6,7},{7,8},{8,9},{9,10},{10,1... | collective-permute-start | bytes 3080 | tf_op jit(solution)/shard_map/ppermute | solution.py:14
  37.7 39.2 %copy-start.5 = (bf16[24,16,16,16]{0,3,2,1:T(8,128)(2,1)S(1)}, bf16[24,16,16,16]{0,3,2,1:T(8,128)(2,1)}, u32[]{:S(2)}) copy-start(bf16[24,16,16,16]{0,3,2,1:T(8,128)(2,1)} %param.21) | copy-start | bytes 589828
  93.5 57.6 %copy-start.2 = (bf16[512,16,32]{2,1,0:T(8,128)(2,1)S(1)}, bf16[512,16,32]{2,1,0:T(8,128)(2,1)}, u32[]{:S(2)}) copy-start(bf16[512,16,32]{2,1,0:T(8,128)(2,1)} %all_gather.15) | copy-start | bytes 1572868
  151.5 5.2 %copy-start.1 = (bf16[3584,16,32]{2,1,0:T(8,128)(2,1)}, bf16[3584,16,32]{2,1,0:T(8,128)(2,1)S(1)}, u32[]{:S(2)}) copy-start(bf16[3584,16,32]{2,1,0:T(8,128)(2,1)S(1)} %constant_dynamic-update-slice_fusion) | copy-start | bytes 11010052
  192.1 8.2 %copy-start.6 = (f32[24,32,128]{2,1,0:T(8,128)S(1)}, f32[24,32,128]{2,1,0:T(8,128)}, u32[]{:S(2)}) copy-start(f32[24,32,128]{2,1,0:T(8,128)} %fusion.6) | copy-start | bytes 1179652
  192.2 8.2 %copy-start.8 = (bf16[24,16,128]{2,1,0:T(8,128)(2,1)S(1)}, bf16[24,16,128]{2,1,0:T(8,128)(2,1)}, u32[]{:S(2)}) copy-start(bf16[24,16,128]{2,1,0:T(8,128)(2,1)} %param.18) | copy-start | bytes 294916
  200.4 4.0 %copy-start.3 = (bf16[32,16,16,16]{2,1,3,0:T(8,128)(2,1)S(1)}, bf16[32,16,16,16]{2,1,3,0:T(8,128)(2,1)}, u32[]{:S(2)}) copy-start(bf16[32,16,16,16]{2,1,3,0:T(8,128)(2,1)} %copy.84) | copy-start | bytes 786436
Sparse Core Ops, SparseCore 0:
  10.2 54.1 all-gather.2
  67.9 76.2 all-gather.4
where the time goes:
time: 215 us
  local copies, waits for them, and re-layouts  68.8 us (32%)
  waiting for transfers between devices  51.5 us (24%)
  blocking collectives  47.9 us (22%)
  matrix products  21.8 us (10%)
  between operations  15 us (7%)
  starting transfers between devices  5.92 us (3%)
  other arithmetic  3.64 us (2%)
    all_gather x1, waiting for transfers between devices, shards(): cond_table = lax.all_gather(cond_coef, ('net', 'strip'), axis=0, tiled=True)  50.7 us
    all_gather x1, blocking collectives, shards(): iface_table = lax.all_gather(iface_full, 'strip', axis=0, tiled=True)  32.7 us
    dynamic_slice x2, local copies, waits for them, and re-layouts, shards(): lax.dynamic_slice_in_dim(coef_table, net_index * excite_rows, excite_rows...  31.9 us
    unnamed x27, local copies, waits for them, and re-layouts  19.9 us
    all_gather x1, blocking collectives, shards(): iface_full = lax.all_gather(iface_local, 'net', axis=2, tiled=True)  15.3 us
    gather x3, local copies, waits for them, and re-layouts, far_field(): fetched = coef_table[jnp.maximum(source_ids, 0)] * usable[:, :, None, None]  11.7 us
    dot_general x1, matrix products, shards(): jnp.einsum('tkpq,tkrq->trp', near_mat, fetched, preferred_element_type=jn...  8.01 us
    dot_general x2, matrix products, far_field(): jnp.einsum('tap,tar->trp', block_basis, gathered_far, preferred_element_t...  4.8 us
  transfers between devices with their start and end apart: 4, of which 1 were waited for; matrix products, arithmetic and copies ran while one was open for 40% of the time, Pallas kernels for 0%

commit v1 on v0

--- a/solution.py
+++ b/solution.py
@@ -2,6 +2,8 @@
 import jax.numpy as jnp
 from jax import lax
 from jax.sharding import PartitionSpec as P
+
+units_solve = lambda across, vec: jnp.concatenate(jax.lax.all_gather(vec, across), 2)
 
 
 def extended(array, sides, width):
@@ -79,7 +81,7 @@
     )
     cond_coef = coeffs(cond_basis, cond_charge, cond_rank)
     iface_local = coeffs(iface_basis, iface_charge, iface_rank)
-    iface_full = lax.all_gather(iface_local, "net", axis=2, tiled=True)
+    iface_full = units_solve("net", iface_local)
     cond_table = lax.all_gather(cond_coef, ("net", "strip"), axis=0, tiled=True)
     iface_table = lax.all_gather(iface_full, "strip", axis=0, tiled=True)
     coef_table = jnp.concatenate([cond_table, iface_table], 0)

time: 215 us -> 215 us (level)
  no operation moved by 1% of the time
where the time goes in v1:
time: 215 us; the launch traced here: 214 us
  local copies, waits for them, and re-layouts  68.9 us (32%)
  waiting for transfers between devices  51.1 us (24%)
  blocking collectives  48.1 us (22%)
  matrix products  21.8 us (10%)
  between operations  15 us (7%)
  starting transfers between devices  5.92 us (3%)
  other arithmetic  3.64 us (2%)
    all_gather x1, waiting for transfers between devices, shards(): cond_table = lax.all_gather(cond_coef, ('net', 'strip'), axis=0, tiled=True)  50.4 us
    all_gather x1, blocking collectives, shards(): iface_table = lax.all_gather(iface_full, 'strip', axis=0, tiled=True)  32.7 us
    dynamic_slice x2, local copies, waits for them, and re-layouts, shards(): lax.dynamic_slice_in_dim(coef_table, net_index * excite_rows, excite_rows...  31.9 us
    unnamed x27, local copies, waits for them, and re-layouts  19.9 us
    all_gather x1, blocking collectives, jax.lax.all_gather(vec, across)  15.3 us
    gather x3, local copies, waits for them, and re-layouts, far_field(): fetched = coef_table[jnp.maximum(source_ids, 0)] * usable[:, :, None, None]  11.7 us
    dot_general x1, matrix products, shards(): jnp.einsum('tkpq,tkrq->trp', near_mat, fetched, preferred_element_type=jn...  8.02 us
    dot_general x2, matrix products, far_field(): jnp.einsum('tap,tar->trp', block_basis, gathered_far, preferred_element_t...  4.8 us
  transfers between devices with their start and end apart: 4, of which 1 were waited for; matrix products, arithmetic and copies ran while one was open for 40% of the time, Pallas kernels for 0%

profile of v1, /device:TPU:1, one launch (start us, length us, event | category | flops | bytes accessed | tf_op | source)
XLA Modules:
  0.0 214.5 jit_solution(8614310691610675653)
XLA Ops:
  7.2 0.0 copy-start
  7.2 0.0 copy-start.7
  7.2 0.0 copy-start.9
  7.2 0.0 copy-start.11
  7.2 0.0 copy-start.10
  7.2 0.0 copy-start.4
  7.2 0.0 all-gather.4.cloned.1.call-start
  7.3 0.7 all-gather.4.cloned.1.call-update
  8.0 0.0 all-gather.6.cloned.1.call-start
  8.0 0.7 fusion.50
  8.7 1.8 fusion.19
  10.6 0.0 all-gather.6.cloned.1.call-update
  10.6 0.7 fusion.53
  11.3 1.3 collective-permute-start.1
  12.6 4.6 %collective-permute-start = (bf16[1,4,128]{2,1,0:T(4,128)(2,1)S(1)}, bf16[1,4,128]{2,1,0:T(4,128)(2,1)S(1)}, u32[]{:S(2)}, u32[]{:S(2)}) collective-permute-start(bf16[1,4,128]{2,1,0:T(4,128)(2,1)S(1)} %get-tuple-element.2), channel_id=1, source_target_pairs={{0,1},{1,2},{2,3},{3,4},{4,5},{5,6},{6,7},{7,8},{8,9},{9,10},{10,1... | collective-permute-start | bytes 3080 | tf_op jit(solution)/shard_map/ppermute | solution.py:16
  17.2 0.7 fusion.49
  17.9 0.0 copy-done
  17.9 0.9 fusion.27
  18.8 15.3 %all-gather = bf16[256,16,4]{1,2,0:T(4,128)(2,1)S(1)} all-gather(bf16[32,16,4]{1,2,0:T(4,128)(2,1)S(1)} %fusion.27), channel_id=2, replica_groups=mesh['net'=8,'strip'=16] {'net'}, dimensions={0}, use_global_device_ids=true | all-gather | bytes 36864 | tf_op jit(solution)/shard_map/all_gather | solution.py:6
  34.2 0.2 copy.91
  34.4 0.2 copy.74
  34.6 0.7 broadcast_maximum_fusion
  35.3 0.1 copy.81
  35.4 0.1 reshape.82
  35.4 0.7 broadcast_maximum_fusion.1
  36.1 0.1 copy.75
  36.2 0.1 reshape.74
  36.3 0.7 compare_select_fusion
  37.0 0.1 copy.70
  37.1 0.1 reshape.66
  37.9 0.0 copy-start.5
  37.9 32.7 %all_gather.19 = bf16[512,16,32]{2,1,0:T(8,128)(2,1)} all-gather(bf16[32,16,32]{2,1,0:T(8,128)(2,1)S(1)} %copy.74), channel_id=1, replica_groups=mesh['net'=8,'strip'=16] {'strip'}, dimensions={0}, use_global_device_ids=true | all-gather | bytes 557056 | tf_op jit(solution)/shard_map/all_gather | solution.py:86
  70.6 0.0 copy-done.9
  70.6 0.0 copy-done.10
  70.7 0.0 copy-done.11
  70.7 0.0 copy-done.7
  70.7 1.9 fusion.31
  72.6 0.1 copy.84
  72.6 0.0 copy-done.4
  72.6 4.4 %copy.86 = bf16[32,16,16,16]{2,1,3,0:T(8,128)(2,1)} copy(bf16[32,16,16,16]{0,3,2,1:T(8,128)(2,1)S(1)} %copy-done.4) | data formatting | bytes 524288 | tf_op args[13]
  77.0 0.1 copy.71
  77.1 0.0 copy-done.5
  77.1 3.5 %copy.77 = bf16[24,16,16,16]{3,2,1,0:T(8,128)(2,1)} copy(bf16[24,16,16,16]{0,3,2,1:T(8,128)(2,1)S(1)} %copy-done.5) | data formatting | bytes 393216 | tf_op args[7]
  80.6 0.1 copy.76
  80.6 0.0 collective-permute-done.1
  80.6 1.9 fusion.29
  82.5 3.2 %gather_fusion = bf16[384,32,128]{2,1,0:T(8,128)(2,1)S(1)} fusion(bf16[384,32,128]{2,1,0:T(8,128)(2,1)} %all-gather.4.cloned.1.call-done, s32[1024]{0:T(1024)S(1)} %pad_clamp_fusion.2), kind=kCustom, calls=%fused_computation | custom fusion | bytes 6292992 | tf_op jit(solution)/shard_map/gather | solution.py:67
  85.7 8.0 %fusion.6 = f32[24,32,128]{2,1,0:T(8,128)} fusion(bf16[24,16,128,128]{3,2,1,0:T(8,128)(2,1)} %param.17, bf16[24,16,32,128]{3,2,1,0:T(8,128)(2,1)S(1)} %bitcast.57, bf16[24,16]{1,0:T(8,128)(2,1)S(1)} %copy.71), kind=kOutput, calls=%fused_computation.10 | convolution fusion | flops 404226048 | bytes 16122624 | tf_op jit(solution)/shard_map/tkpq,tkrq->trp/dot_general | solution.py:68
  93.7 50.4 %all-gather.6.cloned.1.call-done = bf16[3072,16,32]{2,1,0:T(8,128)(2,1)} async-done(((bf16[24,16,32]{2,1,0:T(8,128)(2,1)}), bf16[3072,16,32]{2,1,0:T(8,128)(2,1)}) %all-gather.6.cloned.1.call-update) | async-done | bytes 3145744 | tf_op jit(solution)/shard_map/all_gather | solution.py:85
  144.1 6.8 %constant_dynamic-update-slice_fusion.1 = bf16[3584,16,32]{2,1,0:T(8,128)(2,1)S(1)} fusion(bf16[3072,16,32]{2,1,0:T(8,128)(2,1)} %all-gather.6.cloned.1.call-done), kind=kLoop, calls=%fused_computation.58 | loop fusion | bytes 15728640
  151.0 0.0 copy-done.2
  151.0 0.5 constant_dynamic-update-slice_fusion
  151.5 0.0 copy-start.1
  151.5 5.2 %copy-done.1 = bf16[3584,16,32]{2,1,0:T(8,128)(2,1)} copy-done((bf16[3584,16,32]{2,1,0:T(8,128)(2,1)}, bf16[3584,16,32]{2,1,0:T(8,128)(2,1)S(1)}, u32[]{:S(2)}) %copy-start.1) | copy-done | bytes 3670040
  156.7 7.8 %constant_dynamic-slice_fusion = bf16[3584,16,4]{2,1,0:T(8,128)(2,1)} fusion(bf16[3584,16,32]{2,1,0:T(8,128)(2,1)S(1)} %constant_dynamic-update-slice_fusion, s32[]{:T(128)S(6)} %select_n.9), kind=kLoop, calls=%fused_computation.62 | loop fusion | bytes 917508 | tf_op jit(solution)/shard_map/dynamic_slice | solution.py:89
  164.5 24.0 %copy.82 = bf16[3584,16,4]{1,2,0:T(4,128)(2,1)} copy(bf16[3584,16,4]{2,1,0:T(8,128)(2,1)} %constant_dynamic-slice_fusion) | data formatting | bytes 917504 | tf_op jit(solution)/shard_map/dynamic_slice | solution.py:89
  188.6 3.5 %gather_fusion.2 = bf16[512,16,4]{1,2,0:T(4,128)(2,1)S(1)} fusion(bf16[3584,16,4]{1,2,0:T(4,128)(2,1)} %copy.82, s32[1024]{0:T(1024)S(1)} %pad_clamp_fusion), kind=kCustom, calls=%fused_computation.2 | custom fusion | bytes 133120 | tf_op jit(solution)/shard_map/gather | solution.py:32
  192.1 0.0 copy-start.8
  192.1 0.9 copy.92
  193.0 7.2 %gather_fusion.1 = bf16[384,16,32]{2,1,0:T(8,128)(2,1)} fusion(bf16[3584,16,32]{2,1,0:T(8,128)(2,1)} %copy-done.1, s32[1024]{0:T(1024)S(1)} %pad_clamp_fusion.1), kind=kCustom, calls=%fused_computation.1 | custom fusion | bytes 787968 | tf_op jit(solution)/shard_map/gather | solution.py:32
  200.3 3.9 %fusion.9 = bf16[24,32,128]{2,1,0:T(8,128)(2,1)} fusion(f32[24,32,128]{2,1,0:T(8,128)S(1)} %copy-done.6, bf16[24,16,128]{2,1,0:T(8,128)(2,1)S(1)} %copy-done.8, bf16[24,16,16,16]{3,2,1,0:T(8,128)(2,1)} %copy.77, bf16[24,16,16,32]{3,2,1,0:T(8,128)(2,1)} %bitcast.58, bf16[24,16]{1,0:T(8,128)(2,1)S(1)} %copy.76, f32[24]{0:T(128)S(1)} %compare_convert_fusion.3, ...), kind=kOutput, calls=%fused_computation.11 | convolution fusion | flops 10543104 | bytes 1280352 | tf_op jit(solution)/shard_map/tap,tar->trp/dot_general | solution.py:40
  204.2 0.9 fusion.28
  205.1 0.0 collective-permute-done
  205.1 2.5 %fusion.25 = bf16[32,4,128]{2,1,0:T(4,128)(2,1)} fusion(f32[32,4,128]{2,1,0:T(4,128)S(1)} %fusion.28, f32[32,4,128]{2,1,0:T(4,128)S(1)} %fusion.29, f32[32,4,128]{2,1,0:T(4,128)S(1)} %fusion.31, bf16[32,3,128,128]{3,2,1,0:T(8,128)(2,1)} %param.23, bf16[32,4,128]{2,1,0:T(4,128)(2,1)S(1)} %copy-done.7, bf16[1,4,128]{2,1,0:T(4,128)(2,1)S(1)} %collective-permute-done), kind=kOutput, calls=%fused_computation.23 | convolution fusion | flops 4327424 | bytes 1311744 | tf_op jit(solution)/shard_map/tpq,trq->trp/dot_general | solution.py:70
  (15 shorter events, 0.1 us)
Async XLA Ops:
  7.2 10.7 %copy-start = (bf16[32,16,128]{2,1,0:T(8,128)(2,1)S(1)}, bf16[32,16,128]{2,1,0:T(8,128)(2,1)}, u32[]{:S(2)}) copy-start(bf16[32,16,128]{2,1,0:T(8,128)(2,1)} %param.24) | copy-start | bytes 393220
  7.2 63.5 %copy-start.7 = (bf16[32,4,128]{2,1,0:T(4,128)(2,1)S(1)}, bf16[32,4,128]{2,1,0:T(4,128)(2,1)}, u32[]{:S(2)}) copy-start(bf16[32,4,128]{2,1,0:T(4,128)(2,1)} %param.22) | copy-start | bytes 98308
  7.2 63.4 %copy-start.9 = (s32[32,16]{0,1:T(8,128)S(1)}, s32[32,16]{0,1:T(8,128)}, u32[]{:S(2)}) copy-start(s32[32,16]{0,1:T(8,128)} %param.26) | copy-start | bytes 6148
  7.2 63.5 %copy-start.11 = (s32[24,16]{0,1:T(8,128)S(1)}, s32[24,16]{0,1:T(8,128)}, u32[]{:S(2)}) copy-start(s32[24,16]{0,1:T(8,128)} %param.20) | copy-start | bytes 4612
  7.2 63.4 %copy-start.10 = (s32[24,16]{0,1:T(8,128)S(1)}, s32[24,16]{0,1:T(8,128)}, u32[]{:S(2)}) copy-start(s32[24,16]{0,1:T(8,128)} %param.16) | copy-start | bytes 4612
  7.2 65.4 %copy-start.4 = (bf16[32,16,16,16]{0,3,2,1:T(8,128)(2,1)S(1)}, bf16[32,16,16,16]{0,3,2,1:T(8,128)(2,1)}, u32[]{:S(2)}) copy-start(bf16[32,16,16,16]{0,3,2,1:T(8,128)(2,1)} %param.27) | copy-start | bytes 786436
  7.2 75.3 %all-gather.4.cloned.1.call-start = ((), (), s32[]{:S(2)}) async-start(), calls=%async_computation | async-start | bytes 3342336 | tf_op jit(solution)/shard_map/all_gather | solution.py:64
  8.0 136.2 %all-gather.6.cloned.1.call-start = ((), (), s32[]{:S(2)}) async-start(), calls=%async_computation.1 | async-start | bytes 12681216 | tf_op jit(solution)/shard_map/all_gather | solution.py:85
  11.3 69.3 %collective-permute-start.1 = (bf16[1,4,128]{2,1,0:T(4,128)(2,1)S(1)}, bf16[1,4,128]{2,1,0:T(4,128)(2,1)S(1)}, u32[]{:S(2)}, u32[]{:S(2)}) collective-permute-start(bf16[1,4,128]{2,1,0:T(4,128)(2,1)S(1)} %get-tuple-element.3), channel_id=1, source_target_pairs={{1,0},{2,1},{3,2},{4,3},{5,4},{6,5},{7,6},{8,7},{9,8},{10,9},{11,1... | collective-permute-start | bytes 3080 | tf_op jit(solution)/shard_map/ppermute | solution.py:17
  12.6 192.5 %collective-permute-start = (bf16[1,4,128]{2,1,0:T(4,128)(2,1)S(1)}, bf16[1,4,128]{2,1,0:T(4,128)(2,1)S(1)}, u32[]{:S(2)}, u32[]{:S(2)}) collective-permute-start(bf16[1,4,128]{2,1,0:T(4,128)(2,1)S(1)} %get-tuple-element.2), channel_id=1, source_target_pairs={{0,1},{1,2},{2,3},{3,4},{4,5},{5,6},{6,7},{7,8},{8,9},{9,10},{10,1... | collective-permute-start | bytes 3080 | tf_op jit(solution)/shard_map/ppermute | solution.py:16
  37.9 39.2 %copy-start.5 = (bf16[24,16,16,16]{0,3,2,1:T(8,128)(2,1)S(1)}, bf16[24,16,16,16]{0,3,2,1:T(8,128)(2,1)}, u32[]{:S(2)}) copy-start(bf16[24,16,16,16]{0,3,2,1:T(8,128)(2,1)} %param.21) | copy-start | bytes 589828
  93.7 57.2 %copy-start.2 = (bf16[512,16,32]{2,1,0:T(8,128)(2,1)S(1)}, bf16[512,16,32]{2,1,0:T(8,128)(2,1)}, u32[]{:S(2)}) copy-start(bf16[512,16,32]{2,1,0:T(8,128)(2,1)} %all_gather.19) | copy-start | bytes 1572868
  151.5 5.2 %copy-start.1 = (bf16[3584,16,32]{2,1,0:T(8,128)(2,1)}, bf16[3584,16,32]{2,1,0:T(8,128)(2,1)S(1)}, u32[]{:S(2)}) copy-start(bf16[3584,16,32]{2,1,0:T(8,128)(2,1)S(1)} %constant_dynamic-update-slice_fusion) | copy-start | bytes 11010052
  192.1 8.2 %copy-start.6 = (f32[24,32,128]{2,1,0:T(8,128)S(1)}, f32[24,32,128]{2,1,0:T(8,128)}, u32[]{:S(2)}) copy-start(f32[24,32,128]{2,1,0:T(8,128)} %fusion.6) | copy-start | bytes 1179652
  192.1 8.2 %copy-start.8 = (bf16[24,16,128]{2,1,0:T(8,128)(2,1)S(1)}, bf16[24,16,128]{2,1,0:T(8,128)(2,1)}, u32[]{:S(2)}) copy-start(bf16[24,16,128]{2,1,0:T(8,128)(2,1)} %param.18) | copy-start | bytes 294916
  200.3 4.0 %copy-start.3 = (bf16[32,16,16,16]{2,1,3,0:T(8,128)(2,1)S(1)}, bf16[32,16,16,16]{2,1,3,0:T(8,128)(2,1)}, u32[]{:S(2)}) copy-start(bf16[32,16,16,16]{2,1,3,0:T(8,128)(2,1)} %copy.86) | copy-start | bytes 786436
Sparse Core Ops, SparseCore 0:
  10.2 54.0 all-gather.3
  67.9 76.2 all-gather.5
